TPU v7x, 32 devices: a whole 2x2x4 slice. The times are simulated.
32 devices in a mesh: groups: 2 (over y), ep: 16 (over z, x, core), node: 1.
Axes of the slice: x: 2, y: 2, z: 4, core: 2. Of those that a mesh axis runs over, the one named last changes fastest.
Arguments:
- queries: bfloat16 [4096, 64, 576], P(('groups', 'ep'), 'node'), parts along dimension 0, may hold values from -16 to 16
- latent_kv: bfloat16 [4096, 576], P(('groups', 'ep')), parts along dimension 0, may hold values from -4 to 4
- w_value: bfloat16 [64, 512, 128], P('node'), may hold values from -0.25 to 0.25
- moe_tokens: bfloat16 [1024, 4096], P(('groups', 'ep')), parts along dimension 0, may hold values from -6 to 6
- routes: int32 [1024, 8], P(('groups', 'ep')), parts along dimension 0, may hold values from 0 to 15, all different within a row; in each aligned block of 32 rows (0 to 31, 32 to 63, ...) at most 24 rows name the same one
- router: bfloat16 [4096, 16], replicated, may hold values from -0.25 to 0.25
- w_gate: bfloat16 [16, 4096, 2048], P('ep', None, 'node'), may hold values from -0.09375 to 0.09375
- w_up: bfloat16 [16, 4096, 2048], P('ep', None, 'node'), may hold values from -0.09375 to 0.09375
- w_down: bfloat16 [16, 2048, 4096], P('ep', 'node'), may hold values from -0.125 to 0.125
Outputs:
- attention_out: bfloat16 [4096, 8192], P(('groups', 'ep'), 'node'), parts along dimension 0
- moe_out: bfloat16 [1024, 4096], P(('groups', 'ep'), 'node'), parts along dimension 0
There are 2 independent parts, one for each index of `groups`. A program takes and returns all parts, laid end to end along the dimension named above; an argument that names none is the same for every part. Nothing has to cross between parts.
Inputs may be any that keep to these rules, and one draw needn't show every extreme that they name: `routes`: each row names 8 different experts; among the 32 rows of one index of ep no expert is named by more than 24 rows, a bound that some block reaches of them.
All inputs are finite; a program needn't handle non-finite values.
Results may differ from a plain program's by a relative error of at most 0.015.
Values may be sent and summed in bfloat16 or wider, within the bound.
A program may use at most 192 MiB of HBM per device.

v0:
```python
import jax
import jax.numpy as jnp
from jax import lax
from jax.sharding import PartitionSpec as P

ROUTED_SCALE = 2.5
NEGATIVE = -1e30


def attend_block(carry, piece, queries, first_query, scale, latent_width):
    running_max, running_total, context = carry
    query_pos = first_query + lax.iota(jnp.int32, queries.shape[0])
    key_pos = lax.iota(jnp.int32, piece.shape[0])
    visible = key_pos[None, None, :] <= query_pos[:, None, None]
    scores = jnp.einsum("qhc,kc->qhk", queries, piece, preferred_element_type=jnp.float32) * scale
    scores = jnp.where(visible, scores, NEGATIVE)
    new_max = jnp.maximum(running_max, jnp.max(scores, axis=2))
    raised = jnp.where(visible, jnp.exp(scores - new_max[:, :, None]), 0.0)
    new_total = jnp.sum(raised, axis=2)
    values = piece[:, :latent_width]
    added = jnp.einsum(
        "qhk,kc->qhc", raised.astype(jnp.bfloat16), values, preferred_element_type=jnp.float32
    )
    return (new_max, new_total, added)


def per_device(queries, latent_kv, w_value, moe_tokens, routes, router, w_gate, w_up, w_down):
    seq_dev, heads_dev, width = queries.shape
    latent_width = w_value.shape[1]
    value_width = w_value.shape[2]
    scale = (value_width + width - latent_width) ** (-0.5)
    first_query = lax.axis_index("ep") * seq_dev
    start_carry = (
        jnp.full((seq_dev, heads_dev), NEGATIVE, jnp.float32),
        jnp.zeros((seq_dev, heads_dev), jnp.float32),
        jnp.zeros((seq_dev, heads_dev, latent_width), jnp.float32),
    )
    running = attend_block(
        start_carry,
        lax.all_gather(latent_kv, "ep", axis=0, tiled=True),
        queries,
        first_query,
        scale,
        latent_width,
    )
    context = (running[2] / running[1][:, :, None]).astype(jnp.bfloat16)
    attention_out = jnp.einsum("qhc,hcv->qhv", context, w_value, preferred_element_type=jnp.float32)
    attention_out = attention_out.astype(jnp.bfloat16).reshape(seq_dev, heads_dev * value_width)
    tokens_dev, top = routes.shape
    local_experts = w_gate.shape[0]
    ep_size = lax.axis_size("ep")
    experts = local_experts * ep_size
    capacity = min(tokens_dev, 3 * tokens_dev * top // (2 * experts))
    logits = jnp.dot(moe_tokens, router, preferred_element_type=jnp.float32)
    affinity = jax.nn.sigmoid(logits)
    chosen = jnp.take_along_axis(affinity, routes, axis=1)
    gates = ROUTED_SCALE * chosen / jnp.sum(chosen, axis=1, keepdims=True)
    expert_range = lax.iota(jnp.int32, experts)
    member = jnp.any(routes[:, :, None] == expert_range[None, None, :], axis=1).astype(jnp.int32)
    before = jnp.cumsum(member, axis=0) - member
    slots = jnp.take_along_axis(before, routes, axis=1)
    flat_slot = routes * capacity + slots
    token_ids = jnp.broadcast_to(lax.iota(jnp.int32, tokens_dev)[:, None], routes.shape)
    slot_token = (
        jnp.zeros((experts * capacity,), jnp.int32)
        .at[flat_slot.reshape(-1)]
        .set(token_ids.reshape(-1))
    )
    slot_used = jnp.zeros((experts * capacity,), jnp.int32).at[flat_slot.reshape(-1)].set(1)
    outgoing = jnp.where(
        slot_used[:, None] > 0, moe_tokens[slot_token], jnp.zeros((), jnp.bfloat16)
    )
    outgoing = outgoing.reshape(ep_size, local_experts, capacity, moe_tokens.shape[1])
    arrived = lax.all_to_all(outgoing, "ep", split_axis=0, concat_axis=0, tiled=True)
    gate = jnp.einsum("sjcd,jdf->sjcf", arrived, w_gate, preferred_element_type=jnp.float32)
    upward = jnp.einsum("sjcd,jdf->sjcf", arrived, w_up, preferred_element_type=jnp.float32)
    hidden = (jax.nn.silu(gate) * upward).astype(jnp.bfloat16)
    partial_value = jnp.einsum(
        "sjcf,jfd->sjcd", hidden, w_down, preferred_element_type=jnp.float32
    ).astype(jnp.bfloat16)
    returned = lax.all_to_all(partial_value, "ep", split_axis=0, concat_axis=0, tiled=True)
    returned = returned.reshape(experts * capacity, returned.shape[3])
    picked = returned[flat_slot]
    weighted = gates[:, 0:1] * picked[:, 0].astype(jnp.float32)
    for column in range(1, top):
        weighted = weighted + gates[:, column : column + 1] * picked[:, column].astype(jnp.float32)
    moe_out = lax.psum_scatter(
        weighted.astype(jnp.bfloat16), "node", scatter_dimension=1, tiled=True
    )
    return (attention_out, moe_out)


def solution(mesh):
    placed = (
        P(("groups", "ep"), "node", None),
        P(("groups", "ep"), None),
        P("node", None, None),
        P(("groups", "ep"), None),
        P(("groups", "ep"), None),
        P(),
        P("ep", None, "node"),
        P("ep", None, "node"),
        P("ep", "node", None),
    )
    return jax.shard_map(
        per_device,
        mesh=mesh,
        in_specs=placed,
        out_specs=(P(("groups", "ep"), "node"), P(("groups", "ep"), "node")),
        check_vma=False,
    )
```

profile of v0, /device:TPU:11, one launch (start us, length us, event | category | flops | bytes accessed | tf_op | source)
XLA Modules:
  0.0 297.5 jit_solution(10574636322749152898)
XLA Ops:
  7.2 0.7 all-gather.2.cloned.1.call-update
  7.9 0.8 copy.73
  8.7 0.7 fusion.59
  9.6 1.9 gather_fusion.3
  11.9 1.4 scatter_custom_fusion.1
  13.3 1.4 scatter_custom_fusion
  14.9 3.3 %gather_fusion = bf16[384,4096]{1,0:T(8,128)(2,1)S(1)} fusion(bf16[32,4096]{1,0:T(8,128)(2,1)S(1)} %copy-done, s32[1024]{0:T(1024)S(1)} %pad_clamp_fusion.1), kind=kCustom, calls=%fused_computation | custom fusion | bytes 6292992 | tf_op jit(solution)/shard_map/gather | solution.py:71
  18.2 2.0 broadcast_select_fusion
  20.1 6.8 %all-to-all-start = ((bf16[16,1,24,4096]{3,2,1,0:T(8,128)(2,1)}), bf16[16,1,24,4096]{3,2,1,0:T(8,128)(2,1)S(1)}, u32[]{:S(2)}, u32[]{:S(2)}) async-start(bf16[16,1,24,4096]{3,2,1,0:T(8,128)(2,1)} %broadcast_select_fusion), calls=%async_computation | async-start | bytes 6291456 | tf_op jit(solution)/shard_map/all_to_all | solution.py:74
  27.0 1.1 fusion.50
  28.1 2.0 gather_fusion.2
  31.0 0.9 slice_reduce_fusion.7
  32.1 57.9 %all-gather.2.cloned.1.call-done = bf16[2048,576]{0,1:T(8,128)(2,1)} async-done(((bf16[128,576]{0,1:T(8,128)(2,1)}), bf16[2048,576]{0,1:T(8,128)(2,1)}) %all-gather.2.cloned.1.call-update) | async-done | bytes 2359312 | tf_op jit(solution)/shard_map/all_gather | solution.py:40
  90.1 39.7 %fusion = (f32[128,64]{0,1:T(8,128)S(1)}, f32[128,64,2048]{2,0,1:T(8,128)}) fusion(pred[128,2048]{1,0:T(8,128)(4,1)S(1)} %iota_compare_fusion, bf16[128,64,576]{0,2,1:T(8,128)(2,1)} %param.9, bf16[2048,576]{0,1:T(8,128)(2,1)} %all-gather.2.cloned.1.call-done), kind=kOutput, calls=%fused_computation.8 | convolution fusion | flops 19377676288 | bytes 79200256 | tf_op jit(solution)/shard_map/qhc,kc->qhk/dot_general | solution.py:15
  129.8 22.3 %fusion.1 = f32[128,64]{0,1:T(8,128)S(1)} fusion(f32[128,64,2048]{2,0,1:T(8,128)} %get-tuple-element.31, f32[128,64]{0,1:T(8,128)S(1)} %broadcast_maximum_fusion, pred[128,2048]{1,0:T(8,128)(4,1)S(1)} %iota_compare_fusion), kind=kLoop, calls=%fused_computation.9 | loop fusion | flops 83877888 | bytes 67436544 | tf_op jit(solution)/shard_map/reduce_sum | solution.py:19
  152.0 12.2 %fusion.8 = f32[16,24,2048]{2,1,0:T(8,128)} fusion(bf16[1,4096,2048]{2,1,0:T(8,128)(2,1)} %param.16, bf16[16,1,24,4096]{3,2,1,0:T(8,128)(2,1)S(1)} %all-to-all-done), kind=kOutput, calls=%fused_computation.15 | convolution fusion | flops 6442450944 | bytes 23068672 | tf_op jit(solution)/shard_map/sjcd,jdf->sjcf/dot_general | solution.py:76
  164.2 26.7 %fusion.16 = bf16[16,1,24,4096]{3,2,1,0:T(8,128)(2,1)} fusion(bf16[1,2048,4096]{2,1,0:T(8,128)(2,1)} %param.17, f32[16,24,2048]{2,1,0:T(8,128)} %fusion.8, bf16[1,4096,2048]{2,1,0:T(8,128)(2,1)} %param.15, bf16[16,1,24,4096]{3,2,1,0:T(8,128)(2,1)S(1)} %all-to-all-done), kind=kOutput, calls=%fused_computation.22 | convolution fusion | flops 12891193344 | bytes 42991616 | tf_op jit(solution)/shard_map/sjcf,jfd->sjcd/dot_general | solution.py:78
  191.0 8.9 %all-to-all-start.1 = ((bf16[16,1,24,4096]{3,2,1,0:T(8,128)(2,1)}), bf16[16,1,24,4096]{3,2,1,0:T(8,128)(2,1)S(1)}, u32[]{:S(2)}, u32[]{:S(2)}) async-start(bf16[16,1,24,4096]{3,2,1,0:T(8,128)(2,1)} %fusion.16), calls=%async_computation.1 | async-start | bytes 6291456 | tf_op jit(solution)/shard_map/all_to_all | solution.py:81
  199.9 33.1 %fusion.44 = bf16[64,128,128]{1,2,0:T(8,128)(2,1)} fusion(bf16[64,512,128]{2,1,0:T(8,128)(2,1)} %param.11, f32[128,64]{0,1:T(8,128)S(1)} %fusion.1, bf16[2048,576]{0,1:T(8,128)(2,1)} %all-gather.2.cloned.1.call-done, f32[128,64,2048]{2,0,1:T(8,128)} %get-tuple-element.31, f32[128,64]{0,1:T(8,128)S(1)} %broadcast_maximum_fusion, ...), kind=kOutput, calls=%fused_computation.37 | convolution fusion | flops 18346934272 | bytes 80019456 | tf_op jit(solution)/shard_map/qhc,hcv->qhv/dot_general | solution.py:47
  233.1 4.1 %copy.88 = bf16[128,8192]{1,0:T(8,128)(2,1)} copy(bf16[128,8192]{0,1:T(8,128)(2,1)} %bitcast.152) | data formatting | bytes 4194304
  237.1 32.6 %all-to-all-done.1 = bf16[16,1,24,4096]{3,2,1,0:T(8,128)(2,1)S(1)} async-done(((bf16[16,1,24,4096]{3,2,1,0:T(8,128)(2,1)}), bf16[16,1,24,4096]{3,2,1,0:T(8,128)(2,1)S(1)}, u32[]{:S(2)}, u32[]{:S(2)}) %all-to-all-start.1) | async-done | bytes 3145760 | tf_op jit(solution)/shard_map/all_to_all | solution.py:81
  269.7 3.2 %gather_fusion.1 = bf16[256,4096]{1,0:T(8,128)(2,1)} fusion(bf16[384,4096]{1,0:T(8,128)(2,1)S(1)} %bitcast.149, s32[1024]{0:T(1024)S(1)} %copy-done.2), kind=kCustom, calls=%fused_computation.1 | custom fusion | bytes 4195328 | tf_op jit(solution)/shard_map/gather | solution.py:83
  273.0 12.6 %fusion.71 = (bf16[32,1,4096]{2,1,0:T(2,128)(2,1)S(1)}, bf16[32,1,4096]{2,1,0:T(2,128)(2,1)S(1)}, bf16[32,1,4096]{2,1,0:T(2,128)(2,1)S(1)}, bf16[32,1,4096]{2,1,...) fusion(bf16[32,8,4096]{2,1,0:T(8,128)(2,1)} %bitcast.150), kind=kLoop, calls=%fused_computation.101 | loop fusion | bytes 4194304 | tf_op jit(solution)/shard_map/slice | solution.py:84
  285.7 4.8 %fusion.52 = bf16[32,4096]{1,0:T(8,128)(2,1)} fusion(bf16[32,1,4096]{2,1,0:T(2,128)(2,1)S(1)} %get-tuple-element.29, bf16[32,1,4096]{2,1,0:T(2,128)(2,1)S(1)} %get-tuple-element.23, bf16[32,1,4096]{2,1,0:T(2,128)(2,1)S(1)} %get-tuple-element.24, bf16[32,1,4096]{2,1,0:T(2,128)(2,1)S(1)} %get-tuple-element.25, bf16[32,1,4096]{2,1,0:T(2,128)(2,1)S(1)} %get-tuple-element.26, ...), kind=kLoop, calls=%fused_computation.46 | loop fusion | flops 3145728 | bytes 2360320 | tf_op jit(solution)/shard_map/convert_element_type | solution.py:88
  (49 shorter events, 1.9 us)
Async XLA Ops:
  7.2 7.7 %copy-start = (bf16[32,4096]{1,0:T(8,128)(2,1)S(1)}, bf16[32,4096]{1,0:T(8,128)(2,1)}, u32[]{:S(2)}) copy-start(bf16[32,4096]{1,0:T(8,128)(2,1)} %param.12) | copy-start | bytes 786436
  7.2 82.9 %all-gather.2.cloned.1.call-start = ((), (), s32[]{:S(2)}) async-start(), calls=%async_computation.2 | async-start | bytes 2506752 | tf_op jit(solution)/shard_map/all_gather | solution.py:40
  20.1 131.9 %all-to-all-start = ((bf16[16,1,24,4096]{3,2,1,0:T(8,128)(2,1)}), bf16[16,1,24,4096]{3,2,1,0:T(8,128)(2,1)S(1)}, u32[]{:S(2)}, u32[]{:S(2)}) async-start(bf16[16,1,24,4096]{3,2,1,0:T(8,128)(2,1)} %broadcast_select_fusion), calls=%async_computation | async-start | bytes 6291456 | tf_op jit(solution)/shard_map/all_to_all | solution.py:74
  191.0 78.7 %all-to-all-start.1 = ((bf16[16,1,24,4096]{3,2,1,0:T(8,128)(2,1)}), bf16[16,1,24,4096]{3,2,1,0:T(8,128)(2,1)S(1)}, u32[]{:S(2)}, u32[]{:S(2)}) async-start(bf16[16,1,24,4096]{3,2,1,0:T(8,128)(2,1)} %fusion.16), calls=%async_computation.1 | async-start | bytes 6291456 | tf_op jit(solution)/shard_map/all_to_all | solution.py:81
  199.9 69.8 %copy-start.2 = (s32[1024]{0:T(1024)S(1)}, s32[1024]{0:T(1024)}, u32[]{:S(2)}) copy-start(s32[1024]{0:T(1024)} %pad_clamp_fusion) | copy-start | bytes 12292
  269.7 20.7 %copy-start.1 = (bf16[32,4096]{1,0:T(8,128)(2,1)S(1)}, bf16[32,4096]{1,0:T(8,128)(2,1)}, u32[]{:S(2)}) copy-start(bf16[32,4096]{1,0:T(8,128)(2,1)} %param.12) | copy-start | bytes 786436
  272.9 12.7 %copy-start.3 = (f32[32]{0:T(128)S(1)}, f32[32]{0:T(128)}, u32[]{:S(2)}) copy-start(f32[32]{0:T(128)} %get-tuple-element.12) | copy-start | bytes 388
  272.9 12.7 %copy-start.4 = (f32[32]{0:T(128)S(1)}, f32[32]{0:T(128)}, u32[]{:S(2)}) copy-start(f32[32]{0:T(128)} %get-tuple-element.13) | copy-start | bytes 388
  272.9 12.7 %copy-start.5 = (f32[32]{0:T(128)S(1)}, f32[32]{0:T(128)}, u32[]{:S(2)}) copy-start(f32[32]{0:T(128)} %get-tuple-element.14) | copy-start | bytes 388
  272.9 12.7 %copy-start.6 = (f32[32]{0:T(128)S(1)}, f32[32]{0:T(128)}, u32[]{:S(2)}) copy-start(f32[32]{0:T(128)} %get-tuple-element.15) | copy-start | bytes 388
  272.9 12.7 %copy-start.7 = (f32[32]{0:T(128)S(1)}, f32[32]{0:T(128)}, u32[]{:S(2)}) copy-start(f32[32]{0:T(128)} %get-tuple-element.16) | copy-start | bytes 388
  272.9 12.7 %copy-start.8 = (f32[32]{0:T(128)S(1)}, f32[32]{0:T(128)}, u32[]{:S(2)}) copy-start(f32[32]{0:T(128)} %get-tuple-element.17) | copy-start | bytes 388
  273.0 12.7 %copy-start.9 = (f32[32]{0:T(128)S(1)}, f32[32]{0:T(128)}, u32[]{:S(2)}) copy-start(f32[32]{0:T(128)} %get-tuple-element.18) | copy-start | bytes 388
  273.0 12.7 %copy-start.10 = (f32[32]{0:T(128)S(1)}, f32[32]{0:T(128)}, u32[]{:S(2)}) copy-start(f32[32]{0:T(128)} %get-tuple-element.19) | copy-start | bytes 388
Sparse Core Ops, SparseCore 0:
  10.1 79.8 all-gather.1
where the time goes:
time: 302 us; the launch traced here: 297 us
  matrix products  113 us (37%)
  waiting for transfers between devices  91.2 us (30%)
  local copies, waits for them, and re-layouts  32.3 us (11%)
  other arithmetic  30.8 us (10%)
  starting transfers between devices  15.8 us (5%)
  between operations  14.5 us (5%)
    all_gather x1, waiting for transfers between devices, per_device(): lax.all_gather(latent_kv, 'ep', axis=0, tiled=True)  57.9 us
    dot_general x1, matrix products, attend_block(): jnp.einsum('qhc,kc->qhk', queries, piece, preferred_element_type=jnp.floa...  39.7 us
    dot_general x1, matrix products, per_device(): jnp.einsum('qhc,hcv->qhv', context, w_value, preferred_element_type=jnp.f...  33.1 us
    all_to_all x1, waiting for transfers between devices, per_device(): lax.all_to_all(partial_value, 'ep', split_axis=0, concat_axis=0, tiled=True)  32.6 us
    dot_general x1, matrix products, per_device(): jnp.einsum('sjcf,jfd->sjcd', hidden, w_down, preferred_element_type=jnp.f...  26.7 us
    reduce_sum x1, other arithmetic, attend_block(): new_total = jnp.sum(raised, axis=2)  22.3 us
    slice x2, local copies, waits for them, and re-layouts, per_device(): weighted = gates[:, 0:1] * picked[:, 0].astype(jnp.float32)  13.5 us
    dot_general x1, matrix products, per_device(): jnp.einsum('sjcd,jdf->sjcf', arrived, w_up, preferred_element_type=jnp.fl...  12.2 us
  transfers between devices with their start and end apart: 3, of which 2 were waited for; matrix products, arithmetic and copies ran while one was open for 39% of the time, Pallas kernels for 0%

commit v1 on v0

v1 whole, which is shorter than its diff:
```python
import functools

import jax
import jax.numpy as jnp
from jax import lax
from jax.experimental import pallas as pl
from jax.experimental.pallas import tpu as pltpu
from jax.sharding import PartitionSpec as P

ROUTED_SCALE = 2.5
NEGATIVE = -1e30
LOG2E = 1.4426950408889634


def attend_kernel(per_sub, scale, me_ref, q_ref, kv_ref, wv_ref, *rest):
    out_ref = rest[-1]
    heads, seq_dev, width = q_ref.shape
    keys = kv_ref.shape[0]
    latent_width, value_width = wv_ref.shape[1], wv_ref.shape[2]
    first = me_ref[0] * seq_dev
    rows = per_sub * seq_dev
    for sub in range(heads // per_sub):
        q = q_ref[sub * per_sub : (sub + 1) * per_sub].reshape(rows, width)
        scores = lax.dot_general(
            q, kv_ref[...], (((1,), (1,)), ((), ())), preferred_element_type=jnp.float32
        )
        row = lax.broadcasted_iota(jnp.int32, (rows, keys), 0)
        col = lax.broadcasted_iota(jnp.int32, (rows, keys), 1)
        scores = jnp.where(col <= lax.rem(row, seq_dev) + first, scores, NEGATIVE)
        row_max = jnp.max(scores, axis=1, keepdims=True)
        raised = jnp.exp2((scores - row_max) * (scale * LOG2E))
        totals = jnp.sum(raised, axis=1, keepdims=True)
        context = jnp.dot(
            raised.astype(jnp.bfloat16),
            kv_ref[:, :latent_width],
            preferred_element_type=jnp.float32,
        )
        context = (context / totals).astype(jnp.bfloat16)
        for h in range(per_sub):
            head = sub * per_sub + h
            out_ref[:, head * value_width : (head + 1) * value_width] = jnp.dot(
                context[h * seq_dev : (h + 1) * seq_dev],
                wv_ref[head],
                preferred_element_type=jnp.float32,
            ).astype(out_ref.dtype)


def attend(me, q, kv, w_value, start, count, scale, prior):
    heads, seq_dev, width = q.shape
    _, latent_width, value_width = w_value.shape
    keys = kv.shape[0]
    block = min(8, count)
    per_sub = 2 if block % 2 == 0 else 1
    offset = start // block
    in_specs = [
        pl.BlockSpec(memory_space=pltpu.SMEM),
        pl.BlockSpec((block, seq_dev, width), lambda i: (i + offset, 0, 0)),
        pl.BlockSpec((keys, width), lambda i: (0, 0)),
        pl.BlockSpec((block, latent_width, value_width), lambda i: (i + offset, 0, 0)),
    ]
    args = [me, q, kv, w_value]
    aliases = {}
    if prior is not None:
        in_specs.append(pl.BlockSpec(memory_space=pl.ANY))
        args.append(prior)
        aliases = {4: 0}
    return pl.pallas_call(
        functools.partial(attend_kernel, per_sub, scale),
        grid=(count // block,),
        in_specs=in_specs,
        out_specs=pl.BlockSpec((seq_dev, block * value_width), lambda i: (0, i + offset)),
        out_shape=jax.ShapeDtypeStruct((seq_dev, heads * value_width), jnp.bfloat16),
        input_output_aliases=aliases,
        compiler_params=pltpu.CompilerParams(vmem_limit_bytes=56 * 1024 * 1024),
        cost_estimate=pl.CostEstimate(
            flops=2 * count * seq_dev * keys * (width + latent_width),
            bytes_accessed=2 * count * (seq_dev * width + latent_width * value_width),
            transcendentals=count * seq_dev * keys,
        ),
    )(*args)


def per_device(queries, latent_kv, w_value, moe_tokens, routes, router, w_gate, w_up, w_down):
    seq_dev, heads_dev, width = queries.shape
    latent_width, value_width = w_value.shape[1], w_value.shape[2]
    scale = (value_width + width - latent_width) ** (-0.5)
    me = lax.axis_index("ep")
    me_array = jnp.full((1,), me, jnp.int32)
    tokens_dev, top = routes.shape
    local_experts = w_gate.shape[0]
    ep_size = lax.axis_size("ep")
    experts = local_experts * ep_size
    model = moe_tokens.shape[1]
    tokens = tokens_dev * ep_size
    capacity = min(tokens_dev, 3 * tokens_dev * top // (2 * experts))
    slots = capacity * ep_size

    kv = lax.all_gather(latent_kv, "ep", axis=0, tiled=True)
    q = jnp.transpose(queries, (1, 0, 2))

    logits = jnp.dot(moe_tokens, router, preferred_element_type=jnp.float32)
    affinity = jax.nn.sigmoid(logits)
    named = jnp.any(routes[:, :, None] == lax.iota(jnp.int32, experts)[None, None, :], axis=1)
    kept = jnp.where(named, affinity, 0.0)
    gates = ROUTED_SCALE * kept / jnp.sum(kept, axis=1, keepdims=True)
    gate_high = gates.astype(jnp.bfloat16)
    gate_low = (gates - gate_high.astype(jnp.float32)).astype(jnp.bfloat16)
    extra = jnp.concatenate([gate_high, gate_low, named.astype(jnp.bfloat16)], axis=1)
    extra = jnp.pad(extra, ((0, 0), (0, -extra.shape[1] % 128)))
    outgoing = jnp.concatenate([moe_tokens, extra], axis=1)
    kv, outgoing, q = lax.optimization_barrier((kv, outgoing, q))
    packed = lax.all_gather(outgoing, "ep", axis=0, tiled=True)

    half = heads_dev // 2
    attention_out = attend(me_array, q, kv, w_value, 0, half, scale, None)

    packed, attention_out = lax.optimization_barrier((packed, attention_out))
    all_tokens = packed[:, :model]
    extras = packed[:, model:].astype(jnp.float32)
    contributions = jnp.zeros((tokens, model), jnp.float32)
    lower = (lax.iota(jnp.int32, tokens)[:, None] > lax.iota(jnp.int32, tokens)[None, :])
    for j in range(local_experts):
        mine = (lax.iota(jnp.int32, experts) == me * local_experts + j).astype(jnp.float32)
        pick = lambda k: jnp.sum(extras[:, k * experts : (k + 1) * experts] * mine, axis=1)
        gate_of = pick(0) + pick(1)
        member = pick(2)
        rank = jnp.dot(
            lower.astype(jnp.bfloat16),
            member.astype(jnp.bfloat16)[:, None],
            preferred_element_type=jnp.float32,
        )[:, 0].astype(jnp.int32)
        slot = jnp.where(member > 0, rank, -1)
        chosen = (slot[None, :] == lax.iota(jnp.int32, slots)[:, None]).astype(jnp.bfloat16)
        rows = jnp.dot(chosen, all_tokens, preferred_element_type=jnp.float32).astype(jnp.bfloat16)
        gate = jnp.dot(rows, w_gate[j], preferred_element_type=jnp.float32)
        upward = jnp.dot(rows, w_up[j], preferred_element_type=jnp.float32)
        hidden = (jax.nn.silu(gate) * upward).astype(jnp.bfloat16)
        partial_value = jnp.dot(hidden, w_down[j], preferred_element_type=jnp.float32)
        spread = lax.dot_general(
            chosen,
            partial_value.astype(jnp.bfloat16),
            (((0,), (0,)), ((), ())),
            preferred_element_type=jnp.float32,
        )
        contributions = contributions + gate_of[:, None] * spread
    contributions = contributions.astype(jnp.bfloat16)
    moe_out = lax.psum_scatter(contributions, "ep", scatter_dimension=0, tiled=True)
    if lax.axis_size("node") > 1:
        moe_out = lax.psum_scatter(moe_out, "node", scatter_dimension=1, tiled=True)

    contributions, attention_out = lax.optimization_barrier((contributions, attention_out))
    attention_out = attend(
        me_array, q, kv, w_value, half, heads_dev - half, scale, attention_out
    )
    return (attention_out, moe_out)


def solution(mesh):
    placed = (
        P(("groups", "ep"), "node", None),
        P(("groups", "ep"), None),
        P("node", None, None),
        P(("groups", "ep"), None),
        P(("groups", "ep"), None),
        P(),
        P("ep", None, "node"),
        P("ep", None, "node"),
        P("ep", "node", None),
    )
    return jax.shard_map(
        per_device,
        mesh=mesh,
        in_specs=placed,
        out_specs=(P(("groups", "ep"), "node"), P(("groups", "ep"), "node")),
        check_vma=False,
    )
```

time: 302 us -> 237 us (0.78)
  Pallas kernels: 0 us -> 73.9 us
  matrix products: 113 us -> 47 us
  other arithmetic: 30.8 us -> 2.85 us
  starting transfers between devices: 15.8 us -> 0.12 us
  local copies, waits for them, and re-layouts: 32.3 us -> 17.6 us
  waiting for transfers between devices: 91.2 us -> 77.1 us
    pallas_call x0 -> x2, Pallas kernels: none -> 73.9 us  [attend(): pl.pallas_call(functools.partial(attend_kernel, per_sub, scale), grid=(co...]
    dot_general x4 -> x5, matrix products: 112 us -> 45.8 us  [the longest x1 25.1 us: per_device(): jnp.dot(hidden, w_down[j], preferred_element_type=jnp.float32)]
    reduce_scatter x0 -> x1, waiting for transfers between devices: none -> 32.9 us  [per_device(): lax.psum_scatter(contributions, 'ep', scatter_dimension=0, tiled=True)]
    all_to_all x2 -> x0, waiting for transfers between devices: 32.6 us -> none  [the longest x1 32.6 us: per_device(): lax.all_to_all(partial_value, 'ep', split_axis=0, concat_axis=0, tiled=True)]
    reduce_sum x2 -> x1, other arithmetic: 22.4 us -> 0.44 us  [per_device(): jnp.sum(extras[:, k * experts:(k + 1) * experts] * mine, axis=1)]
    all_to_all x2 -> x0, starting transfers between devices: 15.7 us -> none  [the longest x1 8.93 us: per_device(): lax.all_to_all(partial_value, 'ep', split_axis=0, concat_axis=0, tiled=True)]
    all_gather x1 -> x2, waiting for transfers between devices: 57.9 us -> 44.2 us  [the longest x1 28.4 us: per_device(): kv = lax.all_gather(latent_kv, 'ep', axis=0, tiled=True)]
    slice x2 -> x0, local copies, waits for them, and re-layouts: 13.5 us -> none  [per_device(): weighted = gates[:, 0:1] * picked[:, 0].astype(jnp.float32)]
  transfers between devices with their start and end apart: 3 -> 3, of which waited for: 2 -> 3; matrix products, arithmetic and copies ran while one was open for 39% -> 7% of each run, Pallas kernels for 0% -> 32%
where the time goes in v1:
time: 237 us; the launch traced here: 232 us
  waiting for transfers between devices  77.1 us (33%)
  Pallas kernels  73.9 us (31%)
  matrix products  47 us (20%)
  local copies, waits for them, and re-layouts  17.6 us (7%)
  between operations  13.9 us (6%)
  other arithmetic  2.85 us (1%)
    pallas_call x2, Pallas kernels, attend(): pl.pallas_call(functools.partial(attend_kernel, per_sub, scale), grid=(co...  73.9 us
    reduce_scatter x1, waiting for transfers between devices, per_device(): lax.psum_scatter(contributions, 'ep', scatter_dimension=0, tiled=True)  32.9 us
    all_gather x1, waiting for transfers between devices, per_device(): kv = lax.all_gather(latent_kv, 'ep', axis=0, tiled=True)  28.4 us
    dot_general x1, matrix products, per_device(): jnp.dot(hidden, w_down[j], preferred_element_type=jnp.float32)  25.1 us
    unnamed x11, local copies, waits for them, and re-layouts  17.6 us
    all_gather x1, waiting for transfers between devices, per_device(): packed = lax.all_gather(outgoing, 'ep', axis=0, tiled=True)  15.8 us
    dot_general x1, matrix products, per_device(): gate = jnp.dot(rows, w_gate[j], preferred_element_type=jnp.float32)  12 us
  transfers between devices with their start and end apart: 3, of which 3 were waited for; matrix products, arithmetic and copies ran while one was open for 7% of the time, Pallas kernels for 32%

profile of v1, /device:TPU:11, one launch (start us, length us, event | category | flops | bytes accessed | tf_op | source)
XLA Modules:
  0.0 232.4 jit_solution(10023523407280128540)
XLA Ops:
  7.2 0.0 all-gather.3.cloned.1.call-start
  7.2 1.7 copy.16
  9.0 0.0 all-gather.5.cloned.1.call-start
  9.0 0.7 fusion.27
  9.8 1.2 fusion.30
  11.0 0.1 copy.19
  11.1 14.1 %copy.18 = bf16[128,64,576]{2,0,1:T(8,128)(2,1)} copy(bf16[128,64,576]{0,2,1:T(8,128)(2,1)} %param.9) | data formatting | bytes 18874368 | tf_op args[0]
  25.2 0.7 fusion.23
  25.9 28.4 %all-gather.3.cloned.1.call-done.kv_ref = bf16[2048,576]{1,0:T(8,128)(2,1)} async-done(((bf16[128,576]{1,0:T(8,128)(2,1)}), bf16[2048,576]{1,0:T(8,128)(2,1)}) %all-gather.3.cloned.1.call-update) | async-done | bytes 2359312 | tf_op jit(solution)/shard_map/all_gather | solution.py:98
  54.3 0.0 all-gather.5.cloned.1.call-update
  54.3 0.0 reduce-scatter.2.cloned.1.call-start
  54.4 36.9 %shard_map.104.rest_0_ = bf16[128,8192]{1,0:T(8,128)(2,1)} custom-call(s32[1]{0:T(128)} %bitcast.me_ref, bf16[64,128,576]{2,1,0:T(8,128)(2,1)} %bitcast.24, bf16[2048,576]{1,0:T(8,128)(2,1)} %all-gather.3.cloned.1.call-done.kv_ref, bf16[64,512,128]{2,1,0:T(8,128)(2,1)} %wv_ref.3), custom_call_target="tpu_custom_call" | custom-call | flops 18253611008 | bytes 8912896 | tf_op jit(solution)/shard_map/pallas_call | solution.py:67
  91.3 15.8 %all-gather.5.cloned.1.call-done = bf16[512,4224]{1,0:T(8,128)(2,1)} async-done(((bf16[32,4224]{1,0:T(8,128)(2,1)}), bf16[512,4224]{1,0:T(8,128)(2,1)}) %all-gather.5.cloned.1.call-update) | async-done | bytes 4325392 | tf_op jit(solution)/shard_map/all_gather | solution.py:112
  107.0 0.9 slice_convert_fusion
  107.9 0.4 fusion.25
  108.4 0.2 fusion.19
  108.6 4.0 %convolution_convert_fusion = bf16[384,4096]{1,0:T(8,128)(2,1)S(1)} fusion(bf16[512,4224]{1,0:T(8,128)(2,1)} %all-gather.5.cloned.1.call-done, s32[512]{0:T(512)S(1)} %convert_select_fusion), kind=kOutput, calls=%fused_computation.8 | convolution fusion | flops 1612382208 | bytes 7342080 | tf_op jit(solution)/shard_map/dot_general | solution.py:134
  112.7 1.6 copy-done.3
  114.3 12.0 %fusion.4 = f32[384,2048]{1,0:T(8,128)} fusion(bf16[384,4096]{1,0:T(8,128)(2,1)S(1)} %convolution_convert_fusion, bf16[1,4096,2048]{2,1,0:T(8,128)(2,1)} %param.15), kind=kOutput, calls=%fused_computation.4 | convolution fusion | flops 6442450944 | bytes 23068672 | tf_op jit(solution)/shard_map/dot_general | solution.py:135
  126.3 25.1 %fusion.6 = bf16[384,4096]{1,0:T(8,128)(2,1)S(1)} fusion(bf16[1,2048,4096]{2,1,0:T(8,128)(2,1)} %param.17, f32[384,2048]{1,0:T(8,128)} %fusion.4, bf16[384,4096]{1,0:T(8,128)(2,1)} %copy-done.3, bf16[1,4096,2048]{2,1,0:T(8,128)(2,1)} %param.16), kind=kOutput, calls=%fused_computation.7 | convolution fusion | flops 12891193344 | bytes 42991616 | tf_op jit(solution)/shard_map/dot_general | solution.py:138
  151.4 4.5 %multiply_convert_fusion = bf16[512,4096]{1,0:T(8,128)(2,1)} fusion(bf16[384,4096]{1,0:T(8,128)(2,1)S(1)} %fusion.6, f32[512]{0:T(512)S(1)} %add.19, s32[512]{0:T(512)S(1)} %convert_select_fusion), kind=kOutput, calls=%fused_computation.6 | convolution fusion | flops 1615003648 | bytes 7344128 | tf_op jit(solution)/shard_map/dot_general | solution.py:139
  155.9 0.0 reduce-scatter.2.cloned.1.call-update
  155.9 37.1 %shard_map.105 = bf16[128,8192]{1,0:T(8,128)(2,1)} custom-call(s32[1]{0:T(128)} %bitcast.me_ref, bf16[64,128,576]{2,1,0:T(8,128)(2,1)} %bitcast.25, bf16[2048,576]{1,0:T(8,128)(2,1)} %all-gather.3.cloned.1.call-done.kv_ref, bf16[64,512,128]{2,1,0:T(8,128)(2,1)} %wv_ref.3, bf16[128,8192]{1,0:T(8,128)(2,1)} %shard_map.104.rest_0_), custom_call_target="tpu_custom_call", output_to_operand_aliasing={{}: (4, {})} | custom-call | flops 18253611008 | bytes 8912896 | tf_op jit(solution)/shard_map/pallas_call | solution.py:67
  193.0 32.9 %reduce-scatter.2.cloned.1.call-done = bf16[32,4096]{1,0:T(8,128)(2,1)} async-done(((bf16[512,4096]{1,0:T(8,128)(2,1)}), bf16[32,4096]{1,0:T(8,128)(2,1)}) %reduce-scatter.2.cloned.1.call-update) | async-done | bytes 262160 | tf_op jit(solution)/shard_map/reduce_scatter | solution.py:147
  (16 shorter events, 0.1 us)
Async XLA Ops:
  7.2 2.6 %copy-start = (bf16[4096,16]{0,1:T(8,128)(2,1)S(1)}, bf16[4096,16]{0,1:T(8,128)(2,1)}, u32[]{:S(2)}) copy-start(bf16[4096,16]{0,1:T(8,128)(2,1)} %param.14) | copy-start | bytes 393220
  7.2 47.1 %all-gather.3.cloned.1.call-start = ((), (), s32[]{:S(2)}) async-start(), calls=%async_computation.1 | async-start | bytes 2785280 | tf_op jit(solution)/shard_map/all_gather | solution.py:98
  9.0 98.0 %all-gather.5.cloned.1.call-start = ((), (), s32[]{:S(2)}) async-start(), calls=%async_computation.2 | async-start | bytes 4595712 | tf_op jit(solution)/shard_map/all_gather | solution.py:112
  11.1 14.1 %copy-start.2 = (bf16[32,4096]{1,0:T(8,128)(2,1)S(1)}, bf16[32,4096]{1,0:T(8,128)(2,1)}, u32[]{:S(2)}) copy-start(bf16[32,4096]{1,0:T(8,128)(2,1)} %param.12) | copy-start | bytes 786436
  54.3 171.5 %reduce-scatter.2.cloned.1.call-start = ((), (), s32[]{:S(2)}) async-start(), calls=%async_computation.3 | async-start | bytes 4456448 | tf_op jit(solution)/shard_map/reduce_scatter | solution.py:147
  112.7 1.6 copy-start.3
  155.9 70.0 %copy-start.1 = (bf16[4096,16]{0,1:T(8,128)(2,1)S(1)}, bf16[4096,16]{0,1:T(8,128)(2,1)}, u32[]{:S(2)}) copy-start(bf16[4096,16]{0,1:T(8,128)(2,1)} %param.14) | copy-start | bytes 393220
Sparse Core Ops, SparseCore 0:
  10.8 43.4 all-gather.2
  56.6 50.3 all-gather.4
  156.0 69.7 reduce-scatter.1
